TPU v7x, 128 devices: a whole 4x4x4 slice. The times are simulated.
128 devices in a mesh: gz: 16 (over x, y_lo, core), gy: 8 (over y_hi, z).
Axes of the slice: x: 4, y: 4 (y_hi: 2, y_lo: 2; y = y_hi * 2 + y_lo), z: 4, core: 2. Of those that a mesh axis runs over, the one named last changes fastest.
Arguments:
- e_field: float32 [3, 512, 128, 256], P(None, 'gz', 'gy'), may hold values from -6 to 6
- h_field: float32 [3, 512, 128, 256], P(None, 'gz', 'gy'), may hold values from -6 to 6
- e_coef: float32 [512, 128, 256], P('gz', 'gy'), may hold values from 0.14 to 0.55
- e_loss: float32 [512, 128, 256], P('gz', 'gy'), may hold values from 0 to 0.1
- port_cell: int32 [4096], P(('gz', 'gy')), may hold values from 0 to 131071
- port_node: int32 [4096], replicated, may hold values from 0 to 16383
- port_gain: float32 [4096], replicated, may hold values from 0.5 to 2
- diag_blocks: float32 [256, 64, 64], P(('gz', 'gy')), may hold values from -0.5 to 4.5, as said below
- inv_blocks: float32 [256, 64, 64], P(('gz', 'gy')), may hold values from -0.012 to 0.247, as said below
- off_blocks: float32 [256, 4, 64, 64], P(('gz', 'gy')), may hold values from -0.1875 to 0.1875
- off_cols: int32 [256, 4], P(('gz', 'gy')), may hold values from 0 to 255
- volts_init: float32 [16384], P(('gz', 'gy')), may hold values from -6 to 6
Outputs:
- e_final: float32 [3, 512, 128, 256], P(None, 'gz', 'gy')
- h_final: float32 [3, 512, 128, 256], P(None, 'gz', 'gy')
- node_volts: float32 [16384], P(('gz', 'gy'))
Inputs may be any that keep to these rules, and one draw needn't show every extreme that they name: `diag_blocks`: 4 times the identity plus independent entries of spread 1/8. `inv_blocks`: 0.235 times the identity plus small independent entries. `port_cell`: ports may share a cell.
All inputs are finite; a program needn't handle non-finite values.
Results may differ from a plain program's by a relative error of at most 0.00019.
Values sent between devices are 32-bit elements; how exact they have to be, the bound alone decides.
No kernel may reach another device: no remote copies, remote signals or barrier semaphores. Data moves between devices by JAX's collectives and lax.ppermute only.
A program may use at most 64 MiB of HBM per device.

v0:
```python
import jax
import jax.numpy as jnp
from jax import lax
from jax.sharding import PartitionSpec as P

STEPS = 5
NEWTON = 2
BS = 64
NB_DEV = 2
PORT_DEV = 32
precise = lax.Precision.HIGHEST
time_step = 0.55
charge_scale = 4.0
diode_weight = 0.5


def shifted(value, axis, steps):
    count = lax.axis_size(axis)
    first, last = (max(0, -steps), min(count, count - steps))
    return lax.ppermute(value, axis, [(source, source + steps) for source in range(first, last)])


def update_magnetic(e_now, h_now):
    upper_z = shifted(e_now[0:2, 0], "gz", -1)
    upper_y = shifted(jnp.stack([e_now[0, :, 0], e_now[2, :, 0]]), "gy", -1)
    above_z = jnp.concatenate([e_now[0:2, 1:], upper_z[:, None]], axis=1)
    inner_y = jnp.stack([e_now[0, :, 1:], e_now[2, :, 1:]])
    above_y = jnp.concatenate([inner_y, upper_y[:, :, None]], axis=2)
    blank = jnp.zeros((2,) + e_now.shape[1:3] + (1,), jnp.float32)
    above_x = jnp.concatenate([e_now[1:3, :, :, 1:], blank], axis=3)
    curl_x = above_y[1] - e_now[2] - (above_z[1] - e_now[1])
    curl_y = above_z[0] - e_now[0] - (above_x[1] - e_now[2])
    curl_z = above_x[0] - e_now[1] - (above_y[0] - e_now[0])
    return h_now - time_step * jnp.stack([curl_x, curl_y, curl_z])


def update_electric(e_now, h_now, e_coef, e_loss):
    lower_z = shifted(h_now[0:2, -1], "gz", 1)
    lower_y = shifted(jnp.stack([h_now[0, :, -1], h_now[2, :, -1]]), "gy", 1)
    below_z = jnp.concatenate([lower_z[:, None], h_now[0:2, :-1]], axis=1)
    inner_y = jnp.stack([h_now[0, :, :-1], h_now[2, :, :-1]])
    below_y = jnp.concatenate([lower_y[:, :, None], inner_y], axis=2)
    blank = jnp.zeros((2,) + h_now.shape[1:3] + (1,), jnp.float32)
    below_x = jnp.concatenate([blank, h_now[1:3, :, :, :-1]], axis=3)
    back_x = h_now[2] - below_y[1] - (h_now[1] - below_z[1])
    back_y = h_now[0] - below_z[0] - (h_now[2] - below_x[1])
    back_z = h_now[1] - below_x[0] - (h_now[0] - below_y[0])
    return (1.0 - e_loss) * e_now + e_coef * jnp.stack([back_x, back_y, back_z])


def whole_terms(
    volts_all, samples_all, port_node, port_gain, off_blocks, off_cols, own_nodes, first_node
):
    blocks_all = volts_all.reshape(-1, BS)
    picked = blocks_all[off_cols]
    offsum = jnp.einsum("jkab,jkb->ja", off_blocks, picked, precision=precise)
    columns = jnp.arange(NB_DEV * BS, dtype=jnp.int32)
    onehot = ((port_node - first_node)[:, None] == columns[None, :]).astype(jnp.float32)
    inject = jnp.dot(port_gain * samples_all, onehot, precision=precise).reshape(NB_DEV, BS)
    near = volts_all[own_nodes]
    return (offsum, inject, near)


def newton_solve(volts, offsum, inject, diag_blocks, inv_blocks):
    vstart = volts.reshape(NB_DEV, BS)
    target = charge_scale * vstart + inject - offsum
    iterate = vstart
    for newton_round in range(NEWTON):
        resid = (
            jnp.einsum("jab,jb->ja", diag_blocks, iterate, precision=precise)
            + diode_weight * jnp.tanh(iterate)
            - target
        )
        iterate = iterate - jnp.einsum("jab,jb->ja", inv_blocks, resid, precision=precise)
    return iterate.reshape(-1)


def body(
    e_field,
    h_field,
    e_coef,
    e_loss,
    port_cell,
    port_node,
    port_gain,
    diag_blocks,
    inv_blocks,
    off_blocks,
    off_cols,
    volts_init,
):
    device = lax.axis_index(("gz", "gy"))
    first_node = device * (NB_DEV * BS)
    own_nodes = lax.dynamic_slice_in_dim(port_node, device * PORT_DEV, PORT_DEV)
    own_gain = lax.dynamic_slice_in_dim(port_gain, device * PORT_DEV, PORT_DEV)
    coef_flat = e_coef.reshape(-1)
    cell_coef = coef_flat[port_cell]
    depth, height, width = e_coef.shape

    def circuit_inputs(volts, samples):
        volts_all, samples_all = (
            lax.all_gather(volts, ("gz", "gy"), axis=0, tiled=True),
            lax.all_gather(samples, ("gz", "gy"), axis=0, tiled=True),
        )
        return whole_terms(
            volts_all,
            samples_all,
            port_node,
            port_gain,
            off_blocks,
            off_cols,
            own_nodes,
            first_node,
        )

    def advance(step_index, state):
        e_now, h_now, volts, samples = state
        offsum, inject, near = circuit_inputs(volts, samples)
        h_new = update_magnetic(e_now, h_now)
        e_new = update_electric(e_now, h_new, e_coef, e_loss)
        current = own_gain * (samples - near)
        new_z = e_new[2].reshape(-1).at[port_cell].add(-cell_coef * current)
        e_new = jnp.stack([e_new[0], e_new[1], new_z.reshape(depth, height, width)])
        volts_new = newton_solve(volts, offsum, inject, diag_blocks, inv_blocks)
        samples_new = e_new[2].reshape(-1)[port_cell]
        return (e_new, h_new, volts_new, samples_new)

    samples_start = e_field[2].reshape(-1)[port_cell]
    e_end, h_end, volts_end, samples_end = lax.fori_loop(
        0, STEPS, advance, (e_field, h_field, volts_init, samples_start)
    )
    return (e_end, h_end, volts_end)


def solution(mesh):
    placed = (
        P(None, "gz", "gy", None),
        P(None, "gz", "gy", None),
        P("gz", "gy", None),
        P("gz", "gy", None),
        P(("gz", "gy")),
        P(),
        P(),
        P(("gz", "gy"), None, None),
        P(("gz", "gy"), None, None),
        P(("gz", "gy"), None, None, None),
        P(("gz", "gy"), None),
        P(("gz", "gy")),
    )
    return jax.shard_map(
        body,
        mesh=mesh,
        in_specs=placed,
        out_specs=(P(None, "gz", "gy", None), P(None, "gz", "gy", None), P(("gz", "gy"))),
        check_vma=False,
    )
```

profile of v0, /device:TPU:16, one launch (start us, length us, event | category | flops | bytes accessed | tf_op | source)
XLA Modules:
  0.0 2143.5 jit_solution(3278946582006856271)
XLA Ops:
  4.6 2.1 gather_fusion.3
  6.8 2.1 copy.48
  11.0 2130.8 %while.18 = (s32[]{:T(128)}, f32[3,32,16,256]{3,2,1,0:T(8,128)S(1)}, f32[3,32,16,256]{3,2,1,0:T(8,128)S(1)}, f32[128]{0:T(128)S(1)}, f32[32]{0:T(128)}, /*index=...) while((s32[]{:T(128)}, ...), condition=%wide.region_2.0_spmd, body=%wide.region_0.0_spmd.sunk | while | flops 15647837 | bytes 67082616 | solution.py:129
  12.6 5.7 collective-permute-start.1
  25.0 1.9 broadcast_subtract_fusion.4
  26.9 306.8 %all-gather.2 = f32[128,1,128]{2,1,0:T(1,128)S(1)} all-gather(f32[1,1,128]{2,1,0:T(1,128)S(1)} %bitcast.168), channel_id=1, replica_groups=mesh['gz'=16,'gy'=8] {'gz','gy'}, dimensions={0}, use_global_device_ids=true | all-gather | bytes 66048 | tf_op jit(solution)/shard_map/while/body/eval_jaxpr/all_gather | solution.py:102
  338.6 69.4 %all-reduce.4 = f32[4096]{0:T(1024)S(1)} all-reduce(f32[4096]{0:T(1024)S(1)} %dynamic-update-slice.2), channel_id=1, replica_groups=mesh['gz'=16,'gy'=8] {'gz','gy'}, use_global_device_ids=true, to_apply=%add.2 | all-reduce | flops 4096 | bytes 32768 | tf_op jit(solution)/shard_map/while
  424.5 1.9 collective-permute-start.3
  428.2 6.0 collective-permute-done.3
  444.0 1.9 collective-permute-start.1
  452.6 1.9 broadcast_subtract_fusion.4
  454.5 304.1 %all-gather.2 = f32[128,1,128]{2,1,0:T(1,128)S(1)} all-gather(f32[1,1,128]{2,1,0:T(1,128)S(1)} %bitcast.168), channel_id=1, replica_groups=mesh['gz'=16,'gy'=8] {'gz','gy'}, dimensions={0}, use_global_device_ids=true | all-gather | bytes 66048 | tf_op jit(solution)/shard_map/while/body/eval_jaxpr/all_gather | solution.py:102
  763.4 69.4 %all-reduce.4 = f32[4096]{0:T(1024)S(1)} all-reduce(f32[4096]{0:T(1024)S(1)} %dynamic-update-slice.2), channel_id=1, replica_groups=mesh['gz'=16,'gy'=8] {'gz','gy'}, use_global_device_ids=true, to_apply=%add.2 | all-reduce | flops 4096 | bytes 32768 | tf_op jit(solution)/shard_map/while
  849.3 1.9 collective-permute-start.3
  853.1 6.0 collective-permute-done.3
  868.9 1.9 collective-permute-start.1
  879.3 304.1 %all-gather.2 = f32[128,1,128]{2,1,0:T(1,128)S(1)} all-gather(f32[1,1,128]{2,1,0:T(1,128)S(1)} %bitcast.168), channel_id=1, replica_groups=mesh['gz'=16,'gy'=8] {'gz','gy'}, dimensions={0}, use_global_device_ids=true | all-gather | bytes 66048 | tf_op jit(solution)/shard_map/while/body/eval_jaxpr/all_gather | solution.py:102
  1188.3 69.4 %all-reduce.4 = f32[4096]{0:T(1024)S(1)} all-reduce(f32[4096]{0:T(1024)S(1)} %dynamic-update-slice.2), channel_id=1, replica_groups=mesh['gz'=16,'gy'=8] {'gz','gy'}, use_global_device_ids=true, to_apply=%add.2 | all-reduce | flops 4096 | bytes 32768 | tf_op jit(solution)/shard_map/while
  1274.2 1.9 collective-permute-start.3
  1277.9 6.0 collective-permute-done.3
  1293.7 1.9 collective-permute-start.1
  1302.3 1.9 broadcast_subtract_fusion.4
  1304.2 304.1 %all-gather.2 = f32[128,1,128]{2,1,0:T(1,128)S(1)} all-gather(f32[1,1,128]{2,1,0:T(1,128)S(1)} %bitcast.168), channel_id=1, replica_groups=mesh['gz'=16,'gy'=8] {'gz','gy'}, dimensions={0}, use_global_device_ids=true | all-gather | bytes 66048 | tf_op jit(solution)/shard_map/while/body/eval_jaxpr/all_gather | solution.py:102
  1613.1 69.4 %all-reduce.4 = f32[4096]{0:T(1024)S(1)} all-reduce(f32[4096]{0:T(1024)S(1)} %dynamic-update-slice.2), channel_id=1, replica_groups=mesh['gz'=16,'gy'=8] {'gz','gy'}, use_global_device_ids=true, to_apply=%add.2 | all-reduce | flops 4096 | bytes 32768 | tf_op jit(solution)/shard_map/while
  1699.0 1.9 collective-permute-start.3
  1702.8 6.0 collective-permute-done.3
  1718.6 1.9 collective-permute-start.1
  1727.1 1.9 broadcast_subtract_fusion.4
  1729.0 304.1 %all-gather.2 = f32[128,1,128]{2,1,0:T(1,128)S(1)} all-gather(f32[1,1,128]{2,1,0:T(1,128)S(1)} %bitcast.168), channel_id=1, replica_groups=mesh['gz'=16,'gy'=8] {'gz','gy'}, dimensions={0}, use_global_device_ids=true | all-gather | bytes 66048 | tf_op jit(solution)/shard_map/while/body/eval_jaxpr/all_gather | solution.py:102
  2038.0 69.4 %all-reduce.4 = f32[4096]{0:T(1024)S(1)} all-reduce(f32[4096]{0:T(1024)S(1)} %dynamic-update-slice.2), channel_id=1, replica_groups=mesh['gz'=16,'gy'=8] {'gz','gy'}, use_global_device_ids=true, to_apply=%add.2 | all-reduce | flops 4096 | bytes 32768 | tf_op jit(solution)/shard_map/while
  2123.9 1.9 collective-permute-start.3
  2127.6 6.0 collective-permute-done.3
  (486 shorter events, 205.9 us)
Async XLA Ops:
  11.0 322.7 %copy-start.20 = (s32[32]{0:T(128)}, s32[32]{0:T(128)S(1)}, u32[]{:S(2)}) copy-start(s32[32]{0:T(128)S(1)} %get-tuple-element.465) | copy-start | bytes 388 | tf_op jit(solution)/shard_map/while
  12.6 407.6 %collective-permute-start.1 = (f32[2,32,256]{2,1,0:T(8,128)}, f32[2,32,256]{2,1,0:T(8,128)}, u32[]{:S(2)}, u32[]{:S(2)}) collective-permute-start(f32[2,32,256]{2,1,0:T(8,128)} %pad_maximum_fusion.10), channel_id=1, source_target_pairs={{1,0},{2,1},{3,2},{4,3},{5,4},{6,5},{7,6},{9,8},{10,9},{11,10},{12... | collective-permute-start | bytes 196616 | tf_op jit(solution)/shard_map/while/body/eval_jaxpr/ppermute | solution.py:20
  19.0 403.5 %collective-permute-start = (f32[2,16,256]{2,1,0:T(8,128)}, f32[2,16,256]{2,1,0:T(8,128)}, u32[]{:S(2)}, u32[]{:S(2)}) collective-permute-start(f32[2,16,256]{2,1,0:T(8,128)} %slice_bitcast_fusion.7), channel_id=1, source_target_pairs={{8,0},{16,8},{24,16},{32,24},{40,32},{48,40},{56,48},{64,56},{72,6... | collective-permute-start | bytes 98312 | tf_op jit(solution)/shard_map/while/body/eval_jaxpr/ppermute | solution.py:20
  337.0 82.1 %copy-start.17 = (f32[32]{0:T(128)S(1)}, f32[32]{0:T(128)}, u32[]{:S(2)}) copy-start(f32[32]{0:T(128)} %get-tuple-element.467) | copy-start | bytes 388 | tf_op jit(solution)/shard_map/while
  337.0 82.7 %copy-start.9 = (s32[32]{0:T(128)S(1)}, s32[32]{0:T(128)}, u32[]{:S(2)}) copy-start(s32[32]{0:T(128)} %get-tuple-element.409) | copy-start | bytes 388 | tf_op jit(solution)/shard_map/while
  424.5 9.8 collective-permute-start.3
  426.6 7.9 collective-permute-start.2
  442.4 316.1 %copy-start.20 = (s32[32]{0:T(128)}, s32[32]{0:T(128)S(1)}, u32[]{:S(2)}) copy-start(s32[32]{0:T(128)S(1)} %get-tuple-element.465) | copy-start | bytes 388 | tf_op jit(solution)/shard_map/while
  444.0 401.1 %collective-permute-start.1 = (f32[2,32,256]{2,1,0:T(8,128)}, f32[2,32,256]{2,1,0:T(8,128)}, u32[]{:S(2)}, u32[]{:S(2)}) collective-permute-start(f32[2,32,256]{2,1,0:T(8,128)} %pad_maximum_fusion.10), channel_id=1, source_target_pairs={{1,0},{2,1},{3,2},{4,3},{5,4},{6,5},{7,6},{9,8},{10,9},{11,10},{12... | collective-permute-start | bytes 196616 | tf_op jit(solution)/shard_map/while/body/eval_jaxpr/ppermute | solution.py:20
  446.5 400.8 %collective-permute-start = (f32[2,16,256]{2,1,0:T(8,128)}, f32[2,16,256]{2,1,0:T(8,128)}, u32[]{:S(2)}, u32[]{:S(2)}) collective-permute-start(f32[2,16,256]{2,1,0:T(8,128)} %slice_bitcast_fusion.7), channel_id=1, source_target_pairs={{8,0},{16,8},{24,16},{32,24},{40,32},{48,40},{56,48},{64,56},{72,6... | collective-permute-start | bytes 98312 | tf_op jit(solution)/shard_map/while/body/eval_jaxpr/ppermute | solution.py:20
  761.8 82.7 %copy-start.9 = (s32[32]{0:T(128)S(1)}, s32[32]{0:T(128)}, u32[]{:S(2)}) copy-start(s32[32]{0:T(128)} %get-tuple-element.409) | copy-start | bytes 388 | tf_op jit(solution)/shard_map/while
  849.3 9.8 collective-permute-start.3
  851.4 7.9 collective-permute-start.2
  867.3 316.1 %copy-start.20 = (s32[32]{0:T(128)}, s32[32]{0:T(128)S(1)}, u32[]{:S(2)}) copy-start(s32[32]{0:T(128)S(1)} %get-tuple-element.465) | copy-start | bytes 388 | tf_op jit(solution)/shard_map/while
  868.9 401.1 %collective-permute-start.1 = (f32[2,32,256]{2,1,0:T(8,128)}, f32[2,32,256]{2,1,0:T(8,128)}, u32[]{:S(2)}, u32[]{:S(2)}) collective-permute-start(f32[2,32,256]{2,1,0:T(8,128)} %pad_maximum_fusion.10), channel_id=1, source_target_pairs={{1,0},{2,1},{3,2},{4,3},{5,4},{6,5},{7,6},{9,8},{10,9},{11,10},{12... | collective-permute-start | bytes 196616 | tf_op jit(solution)/shard_map/while/body/eval_jaxpr/ppermute | solution.py:20
  871.4 400.8 %collective-permute-start = (f32[2,16,256]{2,1,0:T(8,128)}, f32[2,16,256]{2,1,0:T(8,128)}, u32[]{:S(2)}, u32[]{:S(2)}) collective-permute-start(f32[2,16,256]{2,1,0:T(8,128)} %slice_bitcast_fusion.7), channel_id=1, source_target_pairs={{8,0},{16,8},{24,16},{32,24},{40,32},{48,40},{56,48},{64,56},{72,6... | collective-permute-start | bytes 98312 | tf_op jit(solution)/shard_map/while/body/eval_jaxpr/ppermute | solution.py:20
  1186.7 82.1 %copy-start.17 = (f32[32]{0:T(128)S(1)}, f32[32]{0:T(128)}, u32[]{:S(2)}) copy-start(f32[32]{0:T(128)} %get-tuple-element.467) | copy-start | bytes 388 | tf_op jit(solution)/shard_map/while
  1186.7 82.7 %copy-start.9 = (s32[32]{0:T(128)S(1)}, s32[32]{0:T(128)}, u32[]{:S(2)}) copy-start(s32[32]{0:T(128)} %get-tuple-element.409) | copy-start | bytes 388 | tf_op jit(solution)/shard_map/while
  1274.2 9.8 collective-permute-start.3
  1276.3 7.9 collective-permute-start.2
  1292.1 316.1 %copy-start.20 = (s32[32]{0:T(128)}, s32[32]{0:T(128)S(1)}, u32[]{:S(2)}) copy-start(s32[32]{0:T(128)S(1)} %get-tuple-element.465) | copy-start | bytes 388 | tf_op jit(solution)/shard_map/while
  1293.7 401.1 %collective-permute-start.1 = (f32[2,32,256]{2,1,0:T(8,128)}, f32[2,32,256]{2,1,0:T(8,128)}, u32[]{:S(2)}, u32[]{:S(2)}) collective-permute-start(f32[2,32,256]{2,1,0:T(8,128)} %pad_maximum_fusion.10), channel_id=1, source_target_pairs={{1,0},{2,1},{3,2},{4,3},{5,4},{6,5},{7,6},{9,8},{10,9},{11,10},{12... | collective-permute-start | bytes 196616 | tf_op jit(solution)/shard_map/while/body/eval_jaxpr/ppermute | solution.py:20
  1296.2 400.8 %collective-permute-start = (f32[2,16,256]{2,1,0:T(8,128)}, f32[2,16,256]{2,1,0:T(8,128)}, u32[]{:S(2)}, u32[]{:S(2)}) collective-permute-start(f32[2,16,256]{2,1,0:T(8,128)} %slice_bitcast_fusion.7), channel_id=1, source_target_pairs={{8,0},{16,8},{24,16},{32,24},{40,32},{48,40},{56,48},{64,56},{72,6... | collective-permute-start | bytes 98312 | tf_op jit(solution)/shard_map/while/body/eval_jaxpr/ppermute | solution.py:20
  1611.5 82.7 %copy-start.9 = (s32[32]{0:T(128)S(1)}, s32[32]{0:T(128)}, u32[]{:S(2)}) copy-start(s32[32]{0:T(128)} %get-tuple-element.409) | copy-start | bytes 388 | tf_op jit(solution)/shard_map/while
  1699.0 9.8 collective-permute-start.3
  1701.1 7.9 collective-permute-start.2
  1717.0 316.1 %copy-start.20 = (s32[32]{0:T(128)}, s32[32]{0:T(128)S(1)}, u32[]{:S(2)}) copy-start(s32[32]{0:T(128)S(1)} %get-tuple-element.465) | copy-start | bytes 388 | tf_op jit(solution)/shard_map/while
  1718.6 401.1 %collective-permute-start.1 = (f32[2,32,256]{2,1,0:T(8,128)}, f32[2,32,256]{2,1,0:T(8,128)}, u32[]{:S(2)}, u32[]{:S(2)}) collective-permute-start(f32[2,32,256]{2,1,0:T(8,128)} %pad_maximum_fusion.10), channel_id=1, source_target_pairs={{1,0},{2,1},{3,2},{4,3},{5,4},{6,5},{7,6},{9,8},{10,9},{11,10},{12... | collective-permute-start | bytes 196616 | tf_op jit(solution)/shard_map/while/body/eval_jaxpr/ppermute | solution.py:20
  1721.1 400.8 %collective-permute-start = (f32[2,16,256]{2,1,0:T(8,128)}, f32[2,16,256]{2,1,0:T(8,128)}, u32[]{:S(2)}, u32[]{:S(2)}) collective-permute-start(f32[2,16,256]{2,1,0:T(8,128)} %slice_bitcast_fusion.7), channel_id=1, source_target_pairs={{8,0},{16,8},{24,16},{32,24},{40,32},{48,40},{56,48},{64,56},{72,6... | collective-permute-start | bytes 98312 | tf_op jit(solution)/shard_map/while/body/eval_jaxpr/ppermute | solution.py:20
  2036.4 82.7 %copy-start.9 = (s32[32]{0:T(128)S(1)}, s32[32]{0:T(128)}, u32[]{:S(2)}) copy-start(s32[32]{0:T(128)} %get-tuple-element.409) | copy-start | bytes 388 | tf_op jit(solution)/shard_map/while
  2123.9 9.8 collective-permute-start.3
  2126.0 7.9 collective-permute-start.2
  (66 other events, 1180.0 us)
where the time goes:
time: 2150 us; the launch traced here: 2140 us
  blocking collectives  1870 us (87%)
  local copies, waits for them, and re-layouts  95.4 us (4%)
  other arithmetic  80.4 us (4%)
  starting transfers between devices  37.6 us (2%)
  waiting for transfers between devices  30.2 us (1%)
  matrix products  27.2 us (1%)
    all_gather x5, blocking collectives, circuit_inputs(): lax.all_gather(volts, ('gz', 'gy'), axis=0, tiled=True)  1520 us
    while x5, blocking collectives  347 us
  transfers between devices with their start and end apart: 20, of which 5 were waited for; matrix products, arithmetic and copies ran while one was open for 6% of the time, Pallas kernels for 0%

commit v1 on v0

--- a/solution.py
+++ b/solution.py
@@ -12,6 +12,11 @@
 time_step = 0.55
 charge_scale = 4.0
 diode_weight = 0.5
+
+
+def all_by_exchange(x, axis, along):
+    sent = jnp.stack([x] * lax.axis_size(axis))
+    return jnp.concatenate(lax.all_to_all(sent, axis, 0, 0), axis=along)
 
 
 def shifted(value, axis, steps):
@@ -99,7 +104,7 @@
 
     def circuit_inputs(volts, samples):
         volts_all, samples_all = (
-            lax.all_gather(volts, ("gz", "gy"), axis=0, tiled=True),
+            all_by_exchange(volts, ("gz", "gy"), 0),
             lax.all_gather(samples, ("gz", "gy"), axis=0, tiled=True),
         )
         return whole_terms(

time: 2150 us -> 671 us (0.31)
  blocking collectives: 1870 us -> 329 us
  starting transfers between devices: 37.6 us -> 89.2 us
    all_gather x5 -> x0, blocking collectives: 1520 us -> none  [circuit_inputs(): lax.all_gather(volts, ('gz', 'gy'), axis=0, tiled=True)]
    all_to_all x0 -> x5, starting transfers between devices: none -> 49.8 us  [all_by_exchange(): return jnp.concatenate(lax.all_to_all(sent, axis, 0, 0), axis=along)]
  transfers between devices with their start and end apart: 20 -> 25, of which waited for: 5 -> 5; matrix products, arithmetic and copies ran while one was open for 6% -> 23% of each run, Pallas kernels for 0% -> 0%
where the time goes in v1:
time: 671 us; the launch traced here: 666 us
  blocking collectives  329 us (49%)
  local copies, waits for them, and re-layouts  104 us (15%)
  starting transfers between devices  89.2 us (13%)
  other arithmetic  86.1 us (13%)
  waiting for transfers between devices  28.4 us (4%)
  matrix products  26.5 us (4%)
    while x5, blocking collectives  329 us
    all_to_all x5, starting transfers between devices, all_by_exchange(): return jnp.concatenate(lax.all_to_all(sent, axis, 0, 0), axis=along)  49.8 us
    ppermute x20, starting transfers between devices, shifted(): lax.ppermute(value, axis, [(source, source + steps) for source in range(f...  39.4 us
    ppermute x20, waiting for transfers between devices, shifted(): lax.ppermute(value, axis, [(source, source + steps) for source in range(f...  28.3 us
    while x125, local copies, waits for them, and re-layouts  13.9 us
  transfers between devices with their start and end apart: 25, of which 5 were waited for; matrix products, arithmetic and copies ran while one was open for 23% of the time, Pallas kernels for 0%

profile of v1, /device:TPU:16, one launch (start us, length us, event | category | flops | bytes accessed | tf_op | source)
XLA Modules:
  0.0 666.0 jit_solution(5174719490487856245)
XLA Ops:
  7.4 2.1 copy.48
  11.7 652.6 %while.18 = (s32[]{:T(128)}, f32[3,32,16,256]{3,2,1,0:T(8,128)S(1)}, f32[3,32,16,256]{3,2,1,0:T(8,128)S(1)}, f32[128]{0:T(128)S(1)}, f32[32]{0:T(128)S(1)}, /*in...) while((s32[]{:T(128)}, ...), condition=%wide.region_2.0_spmd, body=%wide.region_0.0_spmd.sunk | while | flops 15647837 | bytes 67406304 | solution.py:134
  13.3 5.7 collective-permute-start.1
  21.6 8.8 %all-to-all-start = ((f32[128,1,128]{2,1,0:T(1,128)}), f32[128,1,128]{2,1,0:T(1,128)S(1)}, u32[]{:S(2)}, u32[]{:S(2)}) async-start(f32[128,1,128]{2,1,0:T(1,128)} %stack.32), calls=%async_computation | async-start | bytes 131072 | tf_op jit(solution)/shard_map/while/body/eval_jaxpr/all_to_all | solution.py:19
  35.3 1.9 broadcast_subtract_fusion.4
  41.7 65.9 %all-reduce.4 = f32[4096]{0:T(1024)S(1)} all-reduce(f32[4096]{0:T(1024)} %dynamic-update-slice.2), channel_id=1, replica_groups=mesh['gz'=16,'gy'=8] {'gz','gy'}, use_global_device_ids=true, to_apply=%add.2 | all-reduce | flops 4096 | bytes 32768 | tf_op jit(solution)/shard_map/while
  126.7 2.5 collective-permute-start.3
  130.8 5.7 collective-permute-done.3
  145.7 1.9 collective-permute-start.1
  150.2 10.2 %all-to-all-start = ((f32[128,1,128]{2,1,0:T(1,128)}), f32[128,1,128]{2,1,0:T(1,128)S(1)}, u32[]{:S(2)}, u32[]{:S(2)}) async-start(f32[128,1,128]{2,1,0:T(1,128)} %stack.32), calls=%async_computation | async-start | bytes 131072 | tf_op jit(solution)/shard_map/while/body/eval_jaxpr/all_to_all | solution.py:19
  165.3 1.9 broadcast_subtract_fusion.4
  171.7 65.9 %all-reduce.4 = f32[4096]{0:T(1024)S(1)} all-reduce(f32[4096]{0:T(1024)} %dynamic-update-slice.2), channel_id=1, replica_groups=mesh['gz'=16,'gy'=8] {'gz','gy'}, use_global_device_ids=true, to_apply=%add.2 | all-reduce | flops 4096 | bytes 32768 | tf_op jit(solution)/shard_map/while
  256.8 2.5 collective-permute-start.3
  260.9 5.7 collective-permute-done.3
  275.8 1.9 collective-permute-start.1
  280.3 10.2 %all-to-all-start = ((f32[128,1,128]{2,1,0:T(1,128)}), f32[128,1,128]{2,1,0:T(1,128)S(1)}, u32[]{:S(2)}, u32[]{:S(2)}) async-start(f32[128,1,128]{2,1,0:T(1,128)} %stack.32), calls=%async_computation | async-start | bytes 131072 | tf_op jit(solution)/shard_map/while/body/eval_jaxpr/all_to_all | solution.py:19
  295.3 1.9 broadcast_subtract_fusion.4
  301.8 65.9 %all-reduce.4 = f32[4096]{0:T(1024)S(1)} all-reduce(f32[4096]{0:T(1024)} %dynamic-update-slice.2), channel_id=1, replica_groups=mesh['gz'=16,'gy'=8] {'gz','gy'}, use_global_device_ids=true, to_apply=%add.2 | all-reduce | flops 4096 | bytes 32768 | tf_op jit(solution)/shard_map/while
  386.8 2.5 collective-permute-start.3
  390.9 5.7 collective-permute-done.3
  405.8 1.9 collective-permute-start.1
  410.3 10.2 %all-to-all-start = ((f32[128,1,128]{2,1,0:T(1,128)}), f32[128,1,128]{2,1,0:T(1,128)S(1)}, u32[]{:S(2)}, u32[]{:S(2)}) async-start(f32[128,1,128]{2,1,0:T(1,128)} %stack.32), calls=%async_computation | async-start | bytes 131072 | tf_op jit(solution)/shard_map/while/body/eval_jaxpr/all_to_all | solution.py:19
  425.4 1.9 broadcast_subtract_fusion.4
  431.8 65.9 %all-reduce.4 = f32[4096]{0:T(1024)S(1)} all-reduce(f32[4096]{0:T(1024)} %dynamic-update-slice.2), channel_id=1, replica_groups=mesh['gz'=16,'gy'=8] {'gz','gy'}, use_global_device_ids=true, to_apply=%add.2 | all-reduce | flops 4096 | bytes 32768 | tf_op jit(solution)/shard_map/while
  516.8 2.5 collective-permute-start.3
  520.9 5.7 collective-permute-done.3
  535.9 1.9 collective-permute-start.1
  540.3 10.2 %all-to-all-start = ((f32[128,1,128]{2,1,0:T(1,128)}), f32[128,1,128]{2,1,0:T(1,128)S(1)}, u32[]{:S(2)}, u32[]{:S(2)}) async-start(f32[128,1,128]{2,1,0:T(1,128)} %stack.32), calls=%async_computation | async-start | bytes 131072 | tf_op jit(solution)/shard_map/while/body/eval_jaxpr/all_to_all | solution.py:19
  555.4 1.9 broadcast_subtract_fusion.4
  561.8 65.9 %all-reduce.4 = f32[4096]{0:T(1024)S(1)} all-reduce(f32[4096]{0:T(1024)} %dynamic-update-slice.2), channel_id=1, replica_groups=mesh['gz'=16,'gy'=8] {'gz','gy'}, use_global_device_ids=true, to_apply=%add.2 | all-reduce | flops 4096 | bytes 32768 | tf_op jit(solution)/shard_map/while
  646.9 2.5 collective-permute-start.3
  651.0 5.7 collective-permute-done.3
  (468 shorter events, 218.6 us)
Async XLA Ops:
  11.7 28.5 %copy-start.14 = (f32[32]{0:T(128)}, f32[32]{0:T(128)S(1)}, u32[]{:S(2)}) copy-start(f32[32]{0:T(128)S(1)} %get-tuple-element.438) | copy-start | bytes 388 | tf_op jit(solution)/shard_map/while
  13.3 109.0 %collective-permute-start.1 = (f32[2,32,256]{2,1,0:T(8,128)}, f32[2,32,256]{2,1,0:T(8,128)}, u32[]{:S(2)}, u32[]{:S(2)}) collective-permute-start(f32[2,32,256]{2,1,0:T(8,128)} %pad_maximum_fusion.10), channel_id=1, source_target_pairs={{1,0},{2,1},{3,2},{4,3},{5,4},{6,5},{7,6},{9,8},{10,9},{11,10},{12... | collective-permute-start | bytes 196616 | tf_op jit(solution)/shard_map/while/body/eval_jaxpr/ppermute | solution.py:25
  19.7 105.1 %collective-permute-start = (f32[2,16,256]{2,1,0:T(8,128)}, f32[2,16,256]{2,1,0:T(8,128)}, u32[]{:S(2)}, u32[]{:S(2)}) collective-permute-start(f32[2,16,256]{2,1,0:T(8,128)} %slice_bitcast_fusion.7), channel_id=1, source_target_pairs={{8,0},{16,8},{24,16},{32,24},{40,32},{48,40},{56,48},{64,56},{72,6... | collective-permute-start | bytes 98312 | tf_op jit(solution)/shard_map/while/body/eval_jaxpr/ppermute | solution.py:25
  21.6 90.0 %all-to-all-start = ((f32[128,1,128]{2,1,0:T(1,128)}), f32[128,1,128]{2,1,0:T(1,128)S(1)}, u32[]{:S(2)}, u32[]{:S(2)}) async-start(f32[128,1,128]{2,1,0:T(1,128)} %stack.32), calls=%async_computation | async-start | bytes 131072 | tf_op jit(solution)/shard_map/while/body/eval_jaxpr/all_to_all | solution.py:19
  108.3 13.3 %copy-start.17 = (f32[32]{0:T(128)S(1)}, f32[32]{0:T(128)}, u32[]{:S(2)}) copy-start(f32[32]{0:T(128)} %get-tuple-element.466) | copy-start | bytes 388 | tf_op jit(solution)/shard_map/while
  126.7 9.8 %collective-permute-start.3 = (f32[2,32,256]{2,1,0:T(8,128)S(1)}, f32[2,32,256]{2,1,0:T(8,128)S(1)}, u32[]{:S(2)}, u32[]{:S(2)}) collective-permute-start(f32[2,32,256]{2,1,0:T(8,128)S(1)} %pad_maximum_fusion.12), channel_id=1, source_target_pairs={{0,1},{1,2},{2,3},{3,4},{4,5},{5,6},{6,7},{8,9},{9,10},{10,11},{11... | collective-permute-start | bytes 196616 | tf_op jit(solution)/shard_map/while/body/eval_jaxpr/ppermute | solution.py:25
  129.4 7.3 %collective-permute-start.2 = (f32[2,16,256]{2,1,0:T(8,128)S(1)}, f32[2,16,256]{2,1,0:T(8,128)S(1)}, u32[]{:S(2)}, u32[]{:S(2)}) collective-permute-start(f32[2,16,256]{2,1,0:T(8,128)S(1)} %slice_bitcast_fusion.9), channel_id=1, source_target_pairs={{0,8},{8,16},{16,24},{24,32},{32,40},{40,48},{48,56},{56,64},{64,7... | collective-permute-start | bytes 98312 | tf_op jit(solution)/shard_map/while/body/eval_jaxpr/ppermute | solution.py:25
  144.2 26.2 %copy-start.14 = (f32[32]{0:T(128)}, f32[32]{0:T(128)S(1)}, u32[]{:S(2)}) copy-start(f32[32]{0:T(128)S(1)} %get-tuple-element.438) | copy-start | bytes 388 | tf_op jit(solution)/shard_map/while
  145.7 106.7 %collective-permute-start.1 = (f32[2,32,256]{2,1,0:T(8,128)}, f32[2,32,256]{2,1,0:T(8,128)}, u32[]{:S(2)}, u32[]{:S(2)}) collective-permute-start(f32[2,32,256]{2,1,0:T(8,128)} %pad_maximum_fusion.10), channel_id=1, source_target_pairs={{1,0},{2,1},{3,2},{4,3},{5,4},{6,5},{7,6},{9,8},{10,9},{11,10},{12... | collective-permute-start | bytes 196616 | tf_op jit(solution)/shard_map/while/body/eval_jaxpr/ppermute | solution.py:25
  148.3 106.5 %collective-permute-start = (f32[2,16,256]{2,1,0:T(8,128)}, f32[2,16,256]{2,1,0:T(8,128)}, u32[]{:S(2)}, u32[]{:S(2)}) collective-permute-start(f32[2,16,256]{2,1,0:T(8,128)} %slice_bitcast_fusion.7), channel_id=1, source_target_pairs={{8,0},{16,8},{24,16},{32,24},{40,32},{48,40},{56,48},{64,56},{72,6... | collective-permute-start | bytes 98312 | tf_op jit(solution)/shard_map/while/body/eval_jaxpr/ppermute | solution.py:25
  150.2 91.5 %all-to-all-start = ((f32[128,1,128]{2,1,0:T(1,128)}), f32[128,1,128]{2,1,0:T(1,128)S(1)}, u32[]{:S(2)}, u32[]{:S(2)}) async-start(f32[128,1,128]{2,1,0:T(1,128)} %stack.32), calls=%async_computation | async-start | bytes 131072 | tf_op jit(solution)/shard_map/while/body/eval_jaxpr/all_to_all | solution.py:19
  238.3 13.3 %copy-start.17 = (f32[32]{0:T(128)S(1)}, f32[32]{0:T(128)}, u32[]{:S(2)}) copy-start(f32[32]{0:T(128)} %get-tuple-element.466) | copy-start | bytes 388 | tf_op jit(solution)/shard_map/while
  256.8 9.8 %collective-permute-start.3 = (f32[2,32,256]{2,1,0:T(8,128)S(1)}, f32[2,32,256]{2,1,0:T(8,128)S(1)}, u32[]{:S(2)}, u32[]{:S(2)}) collective-permute-start(f32[2,32,256]{2,1,0:T(8,128)S(1)} %pad_maximum_fusion.12), channel_id=1, source_target_pairs={{0,1},{1,2},{2,3},{3,4},{4,5},{5,6},{6,7},{8,9},{9,10},{10,11},{11... | collective-permute-start | bytes 196616 | tf_op jit(solution)/shard_map/while/body/eval_jaxpr/ppermute | solution.py:25
  259.5 7.3 %collective-permute-start.2 = (f32[2,16,256]{2,1,0:T(8,128)S(1)}, f32[2,16,256]{2,1,0:T(8,128)S(1)}, u32[]{:S(2)}, u32[]{:S(2)}) collective-permute-start(f32[2,16,256]{2,1,0:T(8,128)S(1)} %slice_bitcast_fusion.9), channel_id=1, source_target_pairs={{0,8},{8,16},{16,24},{24,32},{32,40},{40,48},{48,56},{56,64},{64,7... | collective-permute-start | bytes 98312 | tf_op jit(solution)/shard_map/while/body/eval_jaxpr/ppermute | solution.py:25
  274.2 26.2 %copy-start.14 = (f32[32]{0:T(128)}, f32[32]{0:T(128)S(1)}, u32[]{:S(2)}) copy-start(f32[32]{0:T(128)S(1)} %get-tuple-element.438) | copy-start | bytes 388 | tf_op jit(solution)/shard_map/while
  275.8 106.7 %collective-permute-start.1 = (f32[2,32,256]{2,1,0:T(8,128)}, f32[2,32,256]{2,1,0:T(8,128)}, u32[]{:S(2)}, u32[]{:S(2)}) collective-permute-start(f32[2,32,256]{2,1,0:T(8,128)} %pad_maximum_fusion.10), channel_id=1, source_target_pairs={{1,0},{2,1},{3,2},{4,3},{5,4},{6,5},{7,6},{9,8},{10,9},{11,10},{12... | collective-permute-start | bytes 196616 | tf_op jit(solution)/shard_map/while/body/eval_jaxpr/ppermute | solution.py:25
  278.3 106.5 %collective-permute-start = (f32[2,16,256]{2,1,0:T(8,128)}, f32[2,16,256]{2,1,0:T(8,128)}, u32[]{:S(2)}, u32[]{:S(2)}) collective-permute-start(f32[2,16,256]{2,1,0:T(8,128)} %slice_bitcast_fusion.7), channel_id=1, source_target_pairs={{8,0},{16,8},{24,16},{32,24},{40,32},{48,40},{56,48},{64,56},{72,6... | collective-permute-start | bytes 98312 | tf_op jit(solution)/shard_map/while/body/eval_jaxpr/ppermute | solution.py:25
  280.3 91.5 %all-to-all-start = ((f32[128,1,128]{2,1,0:T(1,128)}), f32[128,1,128]{2,1,0:T(1,128)S(1)}, u32[]{:S(2)}, u32[]{:S(2)}) async-start(f32[128,1,128]{2,1,0:T(1,128)} %stack.32), calls=%async_computation | async-start | bytes 131072 | tf_op jit(solution)/shard_map/while/body/eval_jaxpr/all_to_all | solution.py:19
  386.8 9.8 %collective-permute-start.3 = (f32[2,32,256]{2,1,0:T(8,128)S(1)}, f32[2,32,256]{2,1,0:T(8,128)S(1)}, u32[]{:S(2)}, u32[]{:S(2)}) collective-permute-start(f32[2,32,256]{2,1,0:T(8,128)S(1)} %pad_maximum_fusion.12), channel_id=1, source_target_pairs={{0,1},{1,2},{2,3},{3,4},{4,5},{5,6},{6,7},{8,9},{9,10},{10,11},{11... | collective-permute-start | bytes 196616 | tf_op jit(solution)/shard_map/while/body/eval_jaxpr/ppermute | solution.py:25
  389.5 7.3 %collective-permute-start.2 = (f32[2,16,256]{2,1,0:T(8,128)S(1)}, f32[2,16,256]{2,1,0:T(8,128)S(1)}, u32[]{:S(2)}, u32[]{:S(2)}) collective-permute-start(f32[2,16,256]{2,1,0:T(8,128)S(1)} %slice_bitcast_fusion.9), channel_id=1, source_target_pairs={{0,8},{8,16},{16,24},{24,32},{32,40},{40,48},{48,56},{56,64},{64,7... | collective-permute-start | bytes 98312 | tf_op jit(solution)/shard_map/while/body/eval_jaxpr/ppermute | solution.py:25
  404.2 26.2 %copy-start.14 = (f32[32]{0:T(128)}, f32[32]{0:T(128)S(1)}, u32[]{:S(2)}) copy-start(f32[32]{0:T(128)S(1)} %get-tuple-element.438) | copy-start | bytes 388 | tf_op jit(solution)/shard_map/while
  405.8 106.7 %collective-permute-start.1 = (f32[2,32,256]{2,1,0:T(8,128)}, f32[2,32,256]{2,1,0:T(8,128)}, u32[]{:S(2)}, u32[]{:S(2)}) collective-permute-start(f32[2,32,256]{2,1,0:T(8,128)} %pad_maximum_fusion.10), channel_id=1, source_target_pairs={{1,0},{2,1},{3,2},{4,3},{5,4},{6,5},{7,6},{9,8},{10,9},{11,10},{12... | collective-permute-start | bytes 196616 | tf_op jit(solution)/shard_map/while/body/eval_jaxpr/ppermute | solution.py:25
  408.4 106.5 %collective-permute-start = (f32[2,16,256]{2,1,0:T(8,128)}, f32[2,16,256]{2,1,0:T(8,128)}, u32[]{:S(2)}, u32[]{:S(2)}) collective-permute-start(f32[2,16,256]{2,1,0:T(8,128)} %slice_bitcast_fusion.7), channel_id=1, source_target_pairs={{8,0},{16,8},{24,16},{32,24},{40,32},{48,40},{56,48},{64,56},{72,6... | collective-permute-start | bytes 98312 | tf_op jit(solution)/shard_map/while/body/eval_jaxpr/ppermute | solution.py:25
  410.3 91.5 %all-to-all-start = ((f32[128,1,128]{2,1,0:T(1,128)}), f32[128,1,128]{2,1,0:T(1,128)S(1)}, u32[]{:S(2)}, u32[]{:S(2)}) async-start(f32[128,1,128]{2,1,0:T(1,128)} %stack.32), calls=%async_computation | async-start | bytes 131072 | tf_op jit(solution)/shard_map/while/body/eval_jaxpr/all_to_all | solution.py:19
  516.8 9.8 %collective-permute-start.3 = (f32[2,32,256]{2,1,0:T(8,128)S(1)}, f32[2,32,256]{2,1,0:T(8,128)S(1)}, u32[]{:S(2)}, u32[]{:S(2)}) collective-permute-start(f32[2,32,256]{2,1,0:T(8,128)S(1)} %pad_maximum_fusion.12), channel_id=1, source_target_pairs={{0,1},{1,2},{2,3},{3,4},{4,5},{5,6},{6,7},{8,9},{9,10},{10,11},{11... | collective-permute-start | bytes 196616 | tf_op jit(solution)/shard_map/while/body/eval_jaxpr/ppermute | solution.py:25
  519.5 7.3 %collective-permute-start.2 = (f32[2,16,256]{2,1,0:T(8,128)S(1)}, f32[2,16,256]{2,1,0:T(8,128)S(1)}, u32[]{:S(2)}, u32[]{:S(2)}) collective-permute-start(f32[2,16,256]{2,1,0:T(8,128)S(1)} %slice_bitcast_fusion.9), channel_id=1, source_target_pairs={{0,8},{8,16},{16,24},{24,32},{32,40},{40,48},{48,56},{56,64},{64,7... | collective-permute-start | bytes 98312 | tf_op jit(solution)/shard_map/while/body/eval_jaxpr/ppermute | solution.py:25
  534.3 26.2 %copy-start.14 = (f32[32]{0:T(128)}, f32[32]{0:T(128)S(1)}, u32[]{:S(2)}) copy-start(f32[32]{0:T(128)S(1)} %get-tuple-element.438) | copy-start | bytes 388 | tf_op jit(solution)/shard_map/while
  535.9 106.7 %collective-permute-start.1 = (f32[2,32,256]{2,1,0:T(8,128)}, f32[2,32,256]{2,1,0:T(8,128)}, u32[]{:S(2)}, u32[]{:S(2)}) collective-permute-start(f32[2,32,256]{2,1,0:T(8,128)} %pad_maximum_fusion.10), channel_id=1, source_target_pairs={{1,0},{2,1},{3,2},{4,3},{5,4},{6,5},{7,6},{9,8},{10,9},{11,10},{12... | collective-permute-start | bytes 196616 | tf_op jit(solution)/shard_map/while/body/eval_jaxpr/ppermute | solution.py:25
  538.4 106.5 %collective-permute-start = (f32[2,16,256]{2,1,0:T(8,128)}, f32[2,16,256]{2,1,0:T(8,128)}, u32[]{:S(2)}, u32[]{:S(2)}) collective-permute-start(f32[2,16,256]{2,1,0:T(8,128)} %slice_bitcast_fusion.7), channel_id=1, source_target_pairs={{8,0},{16,8},{24,16},{32,24},{40,32},{48,40},{56,48},{64,56},{72,6... | collective-permute-start | bytes 98312 | tf_op jit(solution)/shard_map/while/body/eval_jaxpr/ppermute | solution.py:25
  540.3 91.5 %all-to-all-start = ((f32[128,1,128]{2,1,0:T(1,128)}), f32[128,1,128]{2,1,0:T(1,128)S(1)}, u32[]{:S(2)}, u32[]{:S(2)}) async-start(f32[128,1,128]{2,1,0:T(1,128)} %stack.32), calls=%async_computation | async-start | bytes 131072 | tf_op jit(solution)/shard_map/while/body/eval_jaxpr/all_to_all | solution.py:19
  646.9 9.8 %collective-permute-start.3 = (f32[2,32,256]{2,1,0:T(8,128)S(1)}, f32[2,32,256]{2,1,0:T(8,128)S(1)}, u32[]{:S(2)}, u32[]{:S(2)}) collective-permute-start(f32[2,32,256]{2,1,0:T(8,128)S(1)} %pad_maximum_fusion.12), channel_id=1, source_target_pairs={{0,1},{1,2},{2,3},{3,4},{4,5},{5,6},{6,7},{8,9},{9,10},{10,11},{11... | collective-permute-start | bytes 196616 | tf_op jit(solution)/shard_map/while/body/eval_jaxpr/ppermute | solution.py:25
  649.6 7.3 %collective-permute-start.2 = (f32[2,16,256]{2,1,0:T(8,128)S(1)}, f32[2,16,256]{2,1,0:T(8,128)S(1)}, u32[]{:S(2)}, u32[]{:S(2)}) collective-permute-start(f32[2,16,256]{2,1,0:T(8,128)S(1)} %slice_bitcast_fusion.9), channel_id=1, source_target_pairs={{0,8},{8,16},{16,24},{24,32},{32,40},{40,48},{48,56},{56,64},{64,7... | collective-permute-start | bytes 98312 | tf_op jit(solution)/shard_map/while/body/eval_jaxpr/ppermute | solution.py:25
  (57 other events, 151.6 us)
